TPU v7x, 256 devices: a whole 4x4x8 slice. The times are simulated.
256 devices in a mesh: ctx: 32 (over z, x_lo, core), head: 8 (over x_hi, y).
Axes of the slice: x: 4 (x_hi: 2, x_lo: 2; x = x_hi * 2 + x_lo), y: 4, z: 8, core: 2. Of those that a mesh axis runs over, the one named last changes fastest.
Arguments:
- queries: bfloat16 [8192, 24, 128], P('ctx', 'head'), may hold values from -4.5 to 4.5, as said below
- key_vectors: bfloat16 [8192, 24, 128], P('ctx', 'head'), may hold values from -4.5 to 4.5, as said below
- value_vectors: bfloat16 [8192, 24, 128], P('ctx', 'head'), may hold values from -6 to 6
- attn_output: bfloat16 [8192, 24, 128], P('ctx', 'head'), may hold values from -6 to 6
- output_grad: bfloat16 [8192, 5120], P('ctx', 'head'), may hold values from -6 to 6
- w_out: bfloat16 [3072, 5120], P('head'), may hold values from -0.078125 to 0.078125
- log_total: float32 [8192, 24], P('ctx', 'head'), as said below
Outputs:
- query_grad: bfloat16 [8192, 24, 128], P('ctx', 'head')
- key_grad: bfloat16 [8192, 24, 128], P('ctx', 'head')
- value_grad: bfloat16 [8192, 24, 128], P('ctx', 'head')
Inputs may be any that keep to these rules, and one draw needn't show every extreme that they name: `queries`: independent entries of order one. `key_vectors`: entries of order one. `log_total`: for each position and head, the log of the sum of exp(scores) over the positions it sees, from the given queries and keys.
All inputs are finite; a program needn't handle non-finite values.
Results may differ from a plain program's by a relative error of at most 0.0058.
Values may be sent and summed in bfloat16 or wider, within the bound.
A program may use at most 128 MiB of HBM per device.

v0:
```python
import jax
import jax.numpy as jnp
from jax import lax
from jax.sharding import PartitionSpec as P


def block_terms(
    query_block,
    grad_block,
    total_block,
    delta_block,
    key_block,
    value_block,
    query_pos,
    key_pos,
    factor,
):
    raw_scores = (
        jnp.einsum("qhd,khd->hqk", query_block, key_block, preferred_element_type=jnp.float32)
        * factor
    )
    visible = key_pos[None, None, :] <= query_pos[None, :, None]
    scores = jnp.where(visible, raw_scores, -jnp.inf)
    prob_full = jnp.exp(scores - total_block[:, :, None])
    prob_grad = jnp.einsum(
        "qhd,khd->hqk", grad_block, value_block, preferred_element_type=jnp.float32
    )
    score_grad = (prob_full * (prob_grad - delta_block[:, :, None])).astype(jnp.bfloat16)
    return (prob_full.astype(jnp.bfloat16), score_grad)


def query_pass(query_group, gathered_keys, gathered_values, span_rows, factor):
    query_rows, grad_rows, total_rows, delta_rows, query_pos = query_group
    highest = jnp.max(query_pos)

    def query_advance(step_index, running):
        offset = step_index * span_rows

        def query_update(query_grad):
            key_block = lax.dynamic_slice_in_dim(gathered_keys, offset, span_rows, 0)
            value_block = lax.dynamic_slice_in_dim(gathered_values, offset, span_rows, 0)
            key_pos = offset + jnp.arange(span_rows, dtype=jnp.int32)
            prob_low, score_grad = block_terms(
                query_rows,
                grad_rows,
                total_rows,
                delta_rows,
                key_block,
                value_block,
                query_pos,
                key_pos,
                factor,
            )
            return (
                query_grad
                + jnp.einsum(
                    "hqk,khd->qhd", score_grad, key_block, preferred_element_type=jnp.float32
                )
                * factor
            )

        return lax.cond(offset <= highest, query_update, lambda carried: carried, running)

    initial = jnp.zeros(query_rows.shape, jnp.float32)
    return lax.fori_loop(0, gathered_keys.shape[0] // span_rows, query_advance, initial)


def key_pass(
    own_keys, own_values, key_pos, all_queries, all_grads, all_totals, all_deltas, span_rows, factor
):
    lowest = jnp.min(key_pos)

    def key_advance(step_index, running):
        offset = step_index * span_rows

        def key_update(carried):
            key_grad, value_grad = carried
            query_block = lax.dynamic_slice_in_dim(all_queries, offset, span_rows, 0)
            grad_block = lax.dynamic_slice_in_dim(all_grads, offset, span_rows, 0)
            total_block = lax.dynamic_slice_in_dim(all_totals, offset, span_rows, 1)
            delta_block = lax.dynamic_slice_in_dim(all_deltas, offset, span_rows, 1)
            query_pos = offset + jnp.arange(span_rows, dtype=jnp.int32)
            prob_low, score_grad = block_terms(
                query_block,
                grad_block,
                total_block,
                delta_block,
                own_keys,
                own_values,
                query_pos,
                key_pos,
                factor,
            )
            key_grad = (
                key_grad
                + jnp.einsum(
                    "hqk,qhd->khd", score_grad, query_block, preferred_element_type=jnp.float32
                )
                * factor
            )
            value_grad = value_grad + jnp.einsum(
                "hqk,qhd->khd", prob_low, grad_block, preferred_element_type=jnp.float32
            )
            return (key_grad, value_grad)

        return lax.cond(
            offset + span_rows - 1 >= lowest, key_update, lambda carried: carried, running
        )

    initial = (jnp.zeros(own_keys.shape, jnp.float32), jnp.zeros(own_values.shape, jnp.float32))
    return lax.fori_loop(0, all_queries.shape[0] // span_rows, key_advance, initial)


def body(queries, key_vectors, value_vectors, attn_output, output_grad, w_out, log_total):
    local_rows, head_count, head_width = queries.shape
    factor = head_width ** (-0.5)
    ctx_count = lax.axis_size("ctx")
    ctx_index = lax.axis_index("ctx")
    total_len = local_rows * ctx_count
    span_rows = min(512, total_len)
    grad_flat = jnp.einsum(
        "tc,rc->tr",
        lax.all_gather(output_grad, "head", axis=1, tiled=True),
        w_out,
        preferred_element_type=jnp.float32,
    )
    attn_grad = grad_flat.astype(jnp.bfloat16).reshape(local_rows, head_count, head_width)
    row_delta = jnp.einsum(
        "qhd,qhd->hq", attn_grad, attn_output, preferred_element_type=jnp.float32
    )
    own_total = jnp.transpose(log_total, (1, 0))
    own_pos = ctx_index * local_rows + jnp.arange(local_rows, dtype=jnp.int32)
    groups = [(queries, attn_grad, own_total, row_delta, own_pos)]
    gathered_keys, gathered_values = (
        lax.all_gather(key_vectors, "ctx", axis=0, tiled=True),
        lax.all_gather(value_vectors, "ctx", axis=0, tiled=True),
    )
    partial_grads = [
        query_pass(query_group, gathered_keys, gathered_values, span_rows, factor)
        for query_group in groups
    ]
    all_queries, all_grads = (
        lax.all_gather(queries, "ctx", axis=0, tiled=True),
        lax.all_gather(attn_grad, "ctx", axis=0, tiled=True),
    )
    all_totals, all_deltas = (
        lax.all_gather(own_total, "ctx", axis=1, tiled=True),
        lax.all_gather(row_delta, "ctx", axis=1, tiled=True),
    )
    key_part, value_part = key_pass(
        key_vectors,
        value_vectors,
        own_pos,
        all_queries,
        all_grads,
        all_totals,
        all_deltas,
        span_rows,
        factor,
    )
    results = [piece.astype(jnp.bfloat16) for piece in partial_grads]
    query_grad = results[0]
    return (query_grad, key_part.astype(jnp.bfloat16), value_part.astype(jnp.bfloat16))


def solution(mesh):
    in_specs = (
        P("ctx", "head", None),
        P("ctx", "head", None),
        P("ctx", "head", None),
        P("ctx", "head", None),
        P("ctx", "head"),
        P("head", None),
        P("ctx", "head"),
    )
    out_specs = (P("ctx", "head", None), P("ctx", "head", None), P("ctx", "head", None))
    return jax.shard_map(body, mesh=mesh, in_specs=in_specs, out_specs=out_specs, check_vma=False)
```

profile of v0, /device:TPU:1, one launch (start us, length us, event | category | flops | bytes accessed | tf_op | source)
XLA Modules:
  0.0 466.0 jit_solution(10017530869229409577)
XLA Ops:
  9.4 67.1 %all-gather.10.cloned.1.call-done = bf16[256,5120]{1,0:T(8,128)(2,1)} async-done(((bf16[256,640]{1,0:T(8,128)(2,1)}), bf16[256,5120]{1,0:T(8,128)(2,1)}) %all-gather.10.cloned.1.call-update) | async-done | bytes 2621456 | tf_op jit(solution)/shard_map/all_gather | solution.py:123
  76.6 4.4 convolution_convert_fusion
  83.8 35.6 %all_gather.25 = f32[3,8192]{1,0:T(4,128)S(1)} all-gather(f32[3,256]{1,0:T(4,128)S(1)} %bitcast.56), channel_id=1, replica_groups=mesh['ctx'=32,'head'=8] {'ctx'}, dimensions={1}, use_global_device_ids=true | all-gather | bytes 101376 | tf_op jit(solution)/shard_map/all_gather | solution.py:147
  121.8 31.2 %all_gather.27 = f32[3,8192]{1,0:T(4,128)S(1)} all-gather(f32[3,256]{1,0:T(4,128)S(1)} %multiply_reduce_fusion), channel_id=1, replica_groups=mesh['ctx'=32,'head'=8] {'ctx'}, dimensions={1}, use_global_device_ids=true | all-gather | bytes 101376 | tf_op jit(solution)/shard_map/all_gather | solution.py:148
  153.0 64.4 %all-gather.8.cloned.1.call-done = bf16[8192,3,128]{2,0,1:T(8,128)(2,1)} async-done(((bf16[256,3,128]{2,0,1:T(8,128)(2,1)}), bf16[8192,3,128]{2,0,1:T(8,128)(2,1)}) %all-gather.8.cloned.1.call-update) | async-done | bytes 6291472 | tf_op jit(solution)/shard_map/all_gather | solution.py:136
  217.4 14.6 %while.37 = (s32[]{:T(128)}, f32[256,3,128]{0,2,1:T(8,128)S(1)}, s32[]{:T(128)}, bf16[8192,3,128]{2,0,1:T(8,128)(2,1)}, bf16[256,3,128]{2,0,1:T(8,128)(2,1)S(1)}...) while((s32[]{:T(128)}, f32[256,3,128]{0,2,1:T(8,128)S(1)}, ...), condition=%wide.region_4.5_spmd.clone, body=%wide.region_1.4_spmd.clone.sunk | while | flops 304677632 | bytes 5782805 | solution.py:65
  218.1 3.5 conditional.6
  219.7 2.0 fusion.10
  232.9 66.2 %all-gather.14.cloned.1.call-done = bf16[8192,3,128]{0,2,1:T(8,128)(2,1)} async-done(((bf16[256,3,128]{0,2,1:T(8,128)(2,1)}), bf16[8192,3,128]{0,2,1:T(8,128)(2,1)}) %all-gather.14.cloned.1.call-update) | async-done | bytes 6291472 | tf_op jit(solution)/shard_map/all_gather | solution.py:144
  299.1 8.6 %copy.36 = bf16[8192,3,128]{2,0,1:T(8,128)(2,1)} copy(bf16[8192,3,128]{0,2,1:T(8,128)(2,1)} %all-gather.14.cloned.1.call-done) | data formatting | bytes 12582912
  307.7 60.7 %all-gather.12.cloned.1.call-done = bf16[8192,3,128]{2,0,1:T(8,128)(2,1)} async-done(((bf16[256,3,128]{2,0,1:T(8,128)(2,1)}), bf16[8192,3,128]{2,0,1:T(8,128)(2,1)}) %all-gather.12.cloned.1.call-update) | async-done | bytes 6291472 | tf_op jit(solution)/shard_map/all_gather | solution.py:143
  368.5 89.4 %while.38 = (s32[]{:T(128)}, f32[256,3,128]{0,2,1:T(8,128)S(1)}, f32[256,3,128]{0,2,1:T(8,128)S(1)}, s32[]{:T(128)}, bf16[8192,3,128]{2,0,1:T(8,128)(2,1)}, /*in...) while((s32[]{:T(128)}, f32[256,3,128]{0,2,1:T(8,128)S(1)}, ...), condition=%wide.region_9.10_spmd.clone, body=%wide.region_6.9_spmd.clone.sunk | while | flops 405832448 | bytes 8566113 | solution.py:111
  369.1 4.9 %conditional.7 = ((f32[256,3,128]{0,2,1:T(8,128)S(1)}, f32[256,3,128]{0,2,1:T(8,128)S(1)})) conditional(s32[]{:T(128)} %convert_element_type.71, (f32[256,3,128]{0,2,1:T(8,128)S(1)}, f32[256,3,128]{0,2,1:T(8,128)S(1)}) %tuple.108, (s32[]{:T(128)}, bf16[8192,3,128]{2,0,1:T(8,128)(2,1)}, s32[]{:T(128)}, bf16[256,3,128]{2,0,1:T(8,128)(2,1)S(1)}, ...), branch_computations={%region_7.7_spmd, %region_8.8_spmd} | conditional | flops 405832448 | bytes 8564814 | solution.py:106
  369.3 1.5 subtract_exponential_fusion
  372.2 1.8 fusion.30
  374.7 4.9 %conditional.7 = ((f32[256,3,128]{0,2,1:T(8,128)S(1)}, f32[256,3,128]{0,2,1:T(8,128)S(1)})) conditional(s32[]{:T(128)} %convert_element_type.71, (f32[256,3,128]{0,2,1:T(8,128)S(1)}, f32[256,3,128]{0,2,1:T(8,128)S(1)}) %tuple.108, (s32[]{:T(128)}, bf16[8192,3,128]{2,0,1:T(8,128)(2,1)}, s32[]{:T(128)}, bf16[256,3,128]{2,0,1:T(8,128)(2,1)S(1)}, ...), branch_computations={%region_7.7_spmd, %region_8.8_spmd} | conditional | flops 405832448 | bytes 8564814 | solution.py:106
  374.9 1.5 subtract_exponential_fusion
  377.8 1.8 fusion.30
  380.3 4.9 %conditional.7 = ((f32[256,3,128]{0,2,1:T(8,128)S(1)}, f32[256,3,128]{0,2,1:T(8,128)S(1)})) conditional(s32[]{:T(128)} %convert_element_type.71, (f32[256,3,128]{0,2,1:T(8,128)S(1)}, f32[256,3,128]{0,2,1:T(8,128)S(1)}) %tuple.108, (s32[]{:T(128)}, bf16[8192,3,128]{2,0,1:T(8,128)(2,1)}, s32[]{:T(128)}, bf16[256,3,128]{2,0,1:T(8,128)(2,1)S(1)}, ...), branch_computations={%region_7.7_spmd, %region_8.8_spmd} | conditional | flops 405832448 | bytes 8564814 | solution.py:106
  380.5 1.5 subtract_exponential_fusion
  383.4 1.8 fusion.30
  385.9 4.9 %conditional.7 = ((f32[256,3,128]{0,2,1:T(8,128)S(1)}, f32[256,3,128]{0,2,1:T(8,128)S(1)})) conditional(s32[]{:T(128)} %convert_element_type.71, (f32[256,3,128]{0,2,1:T(8,128)S(1)}, f32[256,3,128]{0,2,1:T(8,128)S(1)}) %tuple.108, (s32[]{:T(128)}, bf16[8192,3,128]{2,0,1:T(8,128)(2,1)}, s32[]{:T(128)}, bf16[256,3,128]{2,0,1:T(8,128)(2,1)S(1)}, ...), branch_computations={%region_7.7_spmd, %region_8.8_spmd} | conditional | flops 405832448 | bytes 8564814 | solution.py:106
  386.1 1.5 subtract_exponential_fusion
  389.0 1.8 fusion.30
  391.5 4.9 %conditional.7 = ((f32[256,3,128]{0,2,1:T(8,128)S(1)}, f32[256,3,128]{0,2,1:T(8,128)S(1)})) conditional(s32[]{:T(128)} %convert_element_type.71, (f32[256,3,128]{0,2,1:T(8,128)S(1)}, f32[256,3,128]{0,2,1:T(8,128)S(1)}) %tuple.108, (s32[]{:T(128)}, bf16[8192,3,128]{2,0,1:T(8,128)(2,1)}, s32[]{:T(128)}, bf16[256,3,128]{2,0,1:T(8,128)(2,1)S(1)}, ...), branch_computations={%region_7.7_spmd, %region_8.8_spmd} | conditional | flops 405832448 | bytes 8564814 | solution.py:106
  391.7 1.5 subtract_exponential_fusion
  393.2 1.4 fusion.27
  394.6 1.8 fusion.30
  397.1 4.9 %conditional.7 = ((f32[256,3,128]{0,2,1:T(8,128)S(1)}, f32[256,3,128]{0,2,1:T(8,128)S(1)})) conditional(s32[]{:T(128)} %convert_element_type.71, (f32[256,3,128]{0,2,1:T(8,128)S(1)}, f32[256,3,128]{0,2,1:T(8,128)S(1)}) %tuple.108, (s32[]{:T(128)}, bf16[8192,3,128]{2,0,1:T(8,128)(2,1)}, s32[]{:T(128)}, bf16[256,3,128]{2,0,1:T(8,128)(2,1)S(1)}, ...), branch_computations={%region_7.7_spmd, %region_8.8_spmd} | conditional | flops 405832448 | bytes 8564814 | solution.py:106
  397.3 1.5 subtract_exponential_fusion
  400.2 1.8 fusion.30
  402.6 4.9 %conditional.7 = ((f32[256,3,128]{0,2,1:T(8,128)S(1)}, f32[256,3,128]{0,2,1:T(8,128)S(1)})) conditional(s32[]{:T(128)} %convert_element_type.71, (f32[256,3,128]{0,2,1:T(8,128)S(1)}, f32[256,3,128]{0,2,1:T(8,128)S(1)}) %tuple.108, (s32[]{:T(128)}, bf16[8192,3,128]{2,0,1:T(8,128)(2,1)}, s32[]{:T(128)}, bf16[256,3,128]{2,0,1:T(8,128)(2,1)S(1)}, ...), branch_computations={%region_7.7_spmd, %region_8.8_spmd} | conditional | flops 405832448 | bytes 8564814 | solution.py:106
  402.9 1.5 subtract_exponential_fusion
  404.4 1.4 fusion.27
  405.8 1.8 fusion.30
  408.2 4.9 %conditional.7 = ((f32[256,3,128]{0,2,1:T(8,128)S(1)}, f32[256,3,128]{0,2,1:T(8,128)S(1)})) conditional(s32[]{:T(128)} %convert_element_type.71, (f32[256,3,128]{0,2,1:T(8,128)S(1)}, f32[256,3,128]{0,2,1:T(8,128)S(1)}) %tuple.108, (s32[]{:T(128)}, bf16[8192,3,128]{2,0,1:T(8,128)(2,1)}, s32[]{:T(128)}, bf16[256,3,128]{2,0,1:T(8,128)(2,1)S(1)}, ...), branch_computations={%region_7.7_spmd, %region_8.8_spmd} | conditional | flops 405832448 | bytes 8564814 | solution.py:106
  408.5 1.5 subtract_exponential_fusion
  411.4 1.8 fusion.30
  413.8 4.9 %conditional.7 = ((f32[256,3,128]{0,2,1:T(8,128)S(1)}, f32[256,3,128]{0,2,1:T(8,128)S(1)})) conditional(s32[]{:T(128)} %convert_element_type.71, (f32[256,3,128]{0,2,1:T(8,128)S(1)}, f32[256,3,128]{0,2,1:T(8,128)S(1)}) %tuple.108, (s32[]{:T(128)}, bf16[8192,3,128]{2,0,1:T(8,128)(2,1)}, s32[]{:T(128)}, bf16[256,3,128]{2,0,1:T(8,128)(2,1)S(1)}, ...), branch_computations={%region_7.7_spmd, %region_8.8_spmd} | conditional | flops 405832448 | bytes 8564814 | solution.py:106
  414.0 1.5 subtract_exponential_fusion
  415.6 1.4 fusion.27
  416.9 1.8 fusion.30
  419.4 4.9 %conditional.7 = ((f32[256,3,128]{0,2,1:T(8,128)S(1)}, f32[256,3,128]{0,2,1:T(8,128)S(1)})) conditional(s32[]{:T(128)} %convert_element_type.71, (f32[256,3,128]{0,2,1:T(8,128)S(1)}, f32[256,3,128]{0,2,1:T(8,128)S(1)}) %tuple.108, (s32[]{:T(128)}, bf16[8192,3,128]{2,0,1:T(8,128)(2,1)}, s32[]{:T(128)}, bf16[256,3,128]{2,0,1:T(8,128)(2,1)S(1)}, ...), branch_computations={%region_7.7_spmd, %region_8.8_spmd} | conditional | flops 405832448 | bytes 8564814 | solution.py:106
  419.6 1.5 subtract_exponential_fusion
  422.5 1.8 fusion.30
  425.0 4.9 %conditional.7 = ((f32[256,3,128]{0,2,1:T(8,128)S(1)}, f32[256,3,128]{0,2,1:T(8,128)S(1)})) conditional(s32[]{:T(128)} %convert_element_type.71, (f32[256,3,128]{0,2,1:T(8,128)S(1)}, f32[256,3,128]{0,2,1:T(8,128)S(1)}) %tuple.108, (s32[]{:T(128)}, bf16[8192,3,128]{2,0,1:T(8,128)(2,1)}, s32[]{:T(128)}, bf16[256,3,128]{2,0,1:T(8,128)(2,1)S(1)}, ...), branch_computations={%region_7.7_spmd, %region_8.8_spmd} | conditional | flops 405832448 | bytes 8564814 | solution.py:106
  425.2 1.5 subtract_exponential_fusion
  426.8 1.4 fusion.27
  428.1 1.8 fusion.30
  430.6 4.9 %conditional.7 = ((f32[256,3,128]{0,2,1:T(8,128)S(1)}, f32[256,3,128]{0,2,1:T(8,128)S(1)})) conditional(s32[]{:T(128)} %convert_element_type.71, (f32[256,3,128]{0,2,1:T(8,128)S(1)}, f32[256,3,128]{0,2,1:T(8,128)S(1)}) %tuple.108, (s32[]{:T(128)}, bf16[8192,3,128]{2,0,1:T(8,128)(2,1)}, s32[]{:T(128)}, bf16[256,3,128]{2,0,1:T(8,128)(2,1)S(1)}, ...), branch_computations={%region_7.7_spmd, %region_8.8_spmd} | conditional | flops 405832448 | bytes 8564814 | solution.py:106
  430.8 1.5 subtract_exponential_fusion
  433.7 1.8 fusion.30
  436.2 4.9 %conditional.7 = ((f32[256,3,128]{0,2,1:T(8,128)S(1)}, f32[256,3,128]{0,2,1:T(8,128)S(1)})) conditional(s32[]{:T(128)} %convert_element_type.71, (f32[256,3,128]{0,2,1:T(8,128)S(1)}, f32[256,3,128]{0,2,1:T(8,128)S(1)}) %tuple.108, (s32[]{:T(128)}, bf16[8192,3,128]{2,0,1:T(8,128)(2,1)}, s32[]{:T(128)}, bf16[256,3,128]{2,0,1:T(8,128)(2,1)S(1)}, ...), branch_computations={%region_7.7_spmd, %region_8.8_spmd} | conditional | flops 405832448 | bytes 8564814 | solution.py:106
  436.4 1.5 subtract_exponential_fusion
  439.3 1.8 fusion.30
  441.8 4.9 %conditional.7 = ((f32[256,3,128]{0,2,1:T(8,128)S(1)}, f32[256,3,128]{0,2,1:T(8,128)S(1)})) conditional(s32[]{:T(128)} %convert_element_type.71, (f32[256,3,128]{0,2,1:T(8,128)S(1)}, f32[256,3,128]{0,2,1:T(8,128)S(1)}) %tuple.108, (s32[]{:T(128)}, bf16[8192,3,128]{2,0,1:T(8,128)(2,1)}, s32[]{:T(128)}, bf16[256,3,128]{2,0,1:T(8,128)(2,1)S(1)}, ...), branch_computations={%region_7.7_spmd, %region_8.8_spmd} | conditional | flops 405832448 | bytes 8564814 | solution.py:106
  442.0 1.5 subtract_exponential_fusion
  444.9 1.8 fusion.30
  447.3 4.9 %conditional.7 = ((f32[256,3,128]{0,2,1:T(8,128)S(1)}, f32[256,3,128]{0,2,1:T(8,128)S(1)})) conditional(s32[]{:T(128)} %convert_element_type.71, (f32[256,3,128]{0,2,1:T(8,128)S(1)}, f32[256,3,128]{0,2,1:T(8,128)S(1)}) %tuple.108, (s32[]{:T(128)}, bf16[8192,3,128]{2,0,1:T(8,128)(2,1)}, s32[]{:T(128)}, bf16[256,3,128]{2,0,1:T(8,128)(2,1)S(1)}, ...), branch_computations={%region_7.7_spmd, %region_8.8_spmd} | conditional | flops 405832448 | bytes 8564814 | solution.py:106
  447.6 1.5 subtract_exponential_fusion
  450.5 1.8 fusion.30
  452.9 4.9 %conditional.7 = ((f32[256,3,128]{0,2,1:T(8,128)S(1)}, f32[256,3,128]{0,2,1:T(8,128)S(1)})) conditional(s32[]{:T(128)} %convert_element_type.71, (f32[256,3,128]{0,2,1:T(8,128)S(1)}, f32[256,3,128]{0,2,1:T(8,128)S(1)}) %tuple.108, (s32[]{:T(128)}, bf16[8192,3,128]{2,0,1:T(8,128)(2,1)}, s32[]{:T(128)}, bf16[256,3,128]{2,0,1:T(8,128)(2,1)S(1)}, ...), branch_computations={%region_7.7_spmd, %region_8.8_spmd} | conditional | flops 405832448 | bytes 8564814 | solution.py:106
  453.2 1.5 subtract_exponential_fusion
  456.1 1.8 fusion.30
  (160 shorter events, 30.4 us)
Async XLA Ops:
  7.2 69.4 %all-gather.10.cloned.1.call-start = ((), (), s32[]{:S(2)}) async-start(), calls=%async_computation.2 | async-start | bytes 2949120 | tf_op jit(solution)/shard_map/all_gather | solution.py:123
  7.9 145.1 %all-gather.6.cloned.1.call-start = ((), (), s32[]{:S(2)}) async-start(), calls=%async_computation | async-start | bytes 6488064 | tf_op jit(solution)/shard_map/all_gather | solution.py:135
  8.6 208.7 %all-gather.8.cloned.1.call-start = ((), (), s32[]{:S(2)}) async-start(), calls=%async_computation.1 | async-start | bytes 6488064 | tf_op jit(solution)/shard_map/all_gather | solution.py:136
  9.4 74.4 %copy-start.4 = (f32[256,3]{0,1:T(4,128)S(1)}, f32[256,3]{0,1:T(4,128)}, u32[]{:S(2)}) copy-start(f32[256,3]{0,1:T(4,128)} %param.21) | copy-start | bytes 9220
  9.4 289.7 %all-gather.14.cloned.1.call-start = ((), (), s32[]{:S(2)}) async-start(), calls=%async_computation.4 | async-start | bytes 6488064 | tf_op jit(solution)/shard_map/all_gather | solution.py:144
  81.0 40.6 %copy-start.3 = (bf16[256,3,128]{2,0,1:T(8,128)(2,1)S(1)}, bf16[256,3,128]{2,0,1:T(8,128)(2,1)}, u32[]{:S(2)}) copy-start(bf16[256,3,128]{2,0,1:T(8,128)(2,1)} %param.18) | copy-start | bytes 589828
  81.0 136.4 %copy-start = (bf16[256,3,128]{2,0,1:T(8,128)(2,1)S(1)}, bf16[256,3,128]{2,0,1:T(8,128)(2,1)}, u32[]{:S(2)}) copy-start(bf16[256,3,128]{2,0,1:T(8,128)(2,1)} %param.15) | copy-start | bytes 589828
  81.9 286.5 %all-gather.12.cloned.1.call-start = ((), (), s32[]{:S(2)}) async-start(), calls=%async_computation.3 | async-start | bytes 6488064 | tf_op jit(solution)/shard_map/all_gather | solution.py:143
  232.9 135.6 %copy-start.1 = (bf16[256,3,128]{2,0,1:T(8,128)(2,1)S(1)}, bf16[256,3,128]{2,0,1:T(8,128)(2,1)}, u32[]{:S(2)}) copy-start(bf16[256,3,128]{2,0,1:T(8,128)(2,1)} %param.17) | copy-start | bytes 589828
  232.9 135.6 %copy-start.2 = (bf16[256,3,128]{2,0,1:T(8,128)(2,1)S(1)}, bf16[256,3,128]{2,0,1:T(8,128)(2,1)}, u32[]{:S(2)}) copy-start(bf16[256,3,128]{2,0,1:T(8,128)(2,1)} %param.16) | copy-start | bytes 589828
Sparse Core Ops, SparseCore 0:
  10.7 65.8 all-gather.9
  78.5 68.2 all-gather.5
  148.6 68.7 all-gather.7
  219.6 79.4 all-gather.13
  300.8 67.5 all-gather.11
where the time goes:
time: 468 us; the launch traced here: 466 us
  waiting for transfers between devices  261 us (56%)
  matrix products  82.6 us (18%)
  blocking collectives  66.8 us (14%)
  loops' own time  23 us (5%)
  local copies, waits for them, and re-layouts  14.4 us (3%)
  between operations  13.9 us (3%)
    all_gather x1, waiting for transfers between devices, body(): lax.all_gather(output_grad, 'head', axis=1, tiled=True)  67.1 us
    all_gather x1, waiting for transfers between devices, body(): lax.all_gather(attn_grad, 'ctx', axis=0, tiled=True)  66.2 us
    all_gather x1, waiting for transfers between devices, body(): lax.all_gather(value_vectors, 'ctx', axis=0, tiled=True)  64.4 us
    all_gather x1, waiting for transfers between devices, body(): lax.all_gather(queries, 'ctx', axis=0, tiled=True)  60.7 us
    all_gather x1, blocking collectives, body(): lax.all_gather(own_total, 'ctx', axis=1, tiled=True)  35.6 us
    all_gather x1, blocking collectives, body(): lax.all_gather(row_delta, 'ctx', axis=1, tiled=True)  31.2 us
    dot_general x16, matrix products, key_update(): jnp.einsum('hqk,qhd->khd', score_grad, query_block, preferred_element_typ...  28.6 us
    dot_general x17, matrix products, block_terms(): jnp.einsum('qhd,khd->hqk', query_block, key_block, preferred_element_type...  25.9 us
  transfers between devices with their start and end apart: 5, of which 4 were waited for; matrix products, arithmetic and copies ran while one was open for 5% of the time, Pallas kernels for 0%

commit v1 on v0

--- a/solution.py
+++ b/solution.py
@@ -1,7 +1,18 @@
+import functools
 import jax
 import jax.numpy as jnp
 from jax import lax
 from jax.sharding import PartitionSpec as P
+
+
+def bind_the_lines(x_local, device_axis):
+    then = tuple((x_local for _ in range(lax.axis_size(device_axis))))
+    everything = jnp.stack(then, axis=0)
+    o_now = lax.all_to_all(everything, device_axis, 0, 0)
+    return jnp.concatenate(o_now, axis=1)
+
+
+_connect_classes = functools.partial(bind_the_lines, device_axis="head")
 
 
 def block_terms(
@@ -119,10 +130,7 @@
     total_len = local_rows * ctx_count
     span_rows = min(512, total_len)
     grad_flat = jnp.einsum(
-        "tc,rc->tr",
-        lax.all_gather(output_grad, "head", axis=1, tiled=True),
-        w_out,
-        preferred_element_type=jnp.float32,
+        "tc,rc->tr", _connect_classes(output_grad), w_out, preferred_element_type=jnp.float32
     )
     attn_grad = grad_flat.astype(jnp.bfloat16).reshape(local_rows, head_count, head_width)
     row_delta = jnp.einsum(

time: 468 us -> 411 us (0.88)
  waiting for transfers between devices: 261 us -> 138 us
  blocking collectives: 66.8 us -> 134 us
    all_gather x1 -> x0, waiting for transfers between devices: 67.1 us -> none  [body(): lax.all_gather(output_grad, 'head', axis=1, tiled=True)]
    all_to_all x0 -> x1, blocking collectives: none -> 58.8 us  [bind_the_lines(): o_now = lax.all_to_all(everything, device_axis, 0, 0)]
    all_gather x1, waiting for transfers between devices: 64.4 us -> 8.47 us  [body(): lax.all_gather(value_vectors, 'ctx', axis=0, tiled=True)]
    all_gather x1, blocking collectives: 35.6 us -> 44.1 us  [body(): lax.all_gather(own_total, 'ctx', axis=1, tiled=True)]
    unnamed x13 -> x16, local copies, waits for them, and re-layouts: 10.8 us -> 11.9 us
  transfers between devices with their start and end apart: 5 -> 4, of which waited for: 4 -> 3; matrix products, arithmetic and copies ran while one was open for 5% -> 5% of each run, Pallas kernels for 0% -> 0%
where the time goes in v1:
time: 411 us; the launch traced here: 408 us
  waiting for transfers between devices  138 us (34%)
  blocking collectives  134 us (33%)
  matrix products  80 us (19%)
  loops' own time  22.7 us (6%)
  local copies, waits for them, and re-layouts  15.7 us (4%)
  between operations  13.9 us (3%)
    all_gather x1, waiting for transfers between devices, body(): lax.all_gather(attn_grad, 'ctx', axis=0, tiled=True)  66.3 us
    all_gather x1, waiting for transfers between devices, body(): lax.all_gather(queries, 'ctx', axis=0, tiled=True)  61 us
    all_to_all x1, blocking collectives, bind_the_lines(): o_now = lax.all_to_all(everything, device_axis, 0, 0)  58.8 us
    all_gather x1, blocking collectives, body(): lax.all_gather(own_total, 'ctx', axis=1, tiled=True)  44.1 us
    all_gather x1, blocking collectives, body(): lax.all_gather(row_delta, 'ctx', axis=1, tiled=True)  31.2 us
    dot_general x16, matrix products, key_update(): jnp.einsum('hqk,qhd->khd', score_grad, query_block, preferred_element_typ...  28.8 us
    dot_general x17, matrix products, block_terms(): jnp.einsum('qhd,khd->hqk', query_block, key_block, preferred_element_type...  25.8 us
    dot_general x16, matrix products, key_update(): jnp.einsum('hqk,qhd->khd', prob_low, grad_block, preferred_element_type=j...  21.8 us
  transfers between devices with their start and end apart: 4, of which 3 were waited for; matrix products, arithmetic and copies ran while one was open for 5% of the time, Pallas kernels for 0%

profile of v1, /device:TPU:1, one launch (start us, length us, event | category | flops | bytes accessed | tf_op | source)
XLA Modules:
  0.0 408.4 jit_solution(1738876588022447413)
XLA Ops:
  10.0 58.8 %all_to_all.5 = bf16[8,256,640]{1,2,0:T(8,128)(2,1)S(1)} all-to-all(bf16[8,256,640]{1,2,0:T(8,128)(2,1)S(1)} %stack.2), channel_id=1, replica_groups=mesh['ctx'=32,'head'=8] {'head'}, dimensions={0} | all-to-all | bytes 5242880 | tf_op jit(solution)/shard_map/all_to_all | solution.py:11
  68.9 1.6 convolution_convert_fusion
  73.2 44.1 %all_gather.21 = f32[3,8192]{1,0:T(4,128)S(1)} all-gather(f32[3,256]{1,0:T(4,128)S(1)} %bitcast.60), channel_id=1, replica_groups=mesh['ctx'=32,'head'=8] {'ctx'}, dimensions={1}, use_global_device_ids=true | all-gather | bytes 101376 | tf_op jit(solution)/shard_map/all_gather | solution.py:155
  119.7 31.2 %all_gather.23 = f32[3,8192]{1,0:T(4,128)S(1)} all-gather(f32[3,256]{1,0:T(4,128)S(1)} %multiply_reduce_fusion), channel_id=1, replica_groups=mesh['ctx'=32,'head'=8] {'ctx'}, dimensions={1}, use_global_device_ids=true | all-gather | bytes 101376 | tf_op jit(solution)/shard_map/all_gather | solution.py:156
  150.9 8.5 %all-gather.7.cloned.1.call-done = bf16[8192,3,128]{2,0,1:T(8,128)(2,1)} async-done(((bf16[256,3,128]{2,0,1:T(8,128)(2,1)}), bf16[8192,3,128]{2,0,1:T(8,128)(2,1)}) %all-gather.7.cloned.1.call-update) | async-done | bytes 6291472 | tf_op jit(solution)/shard_map/all_gather | solution.py:144
  159.4 14.6 %while.37 = (s32[]{:T(128)}, f32[256,3,128]{0,2,1:T(8,128)S(1)}, s32[]{:T(128)}, bf16[8192,3,128]{2,0,1:T(8,128)(2,1)}, bf16[256,3,128]{2,0,1:T(8,128)(2,1)S(1)}...) while((s32[]{:T(128)}, f32[256,3,128]{0,2,1:T(8,128)S(1)}, ...), condition=%wide.region_4.5_spmd.clone, body=%wide.region_1.4_spmd.clone.sunk | while | flops 304677632 | bytes 5782805 | solution.py:76
  160.1 3.5 conditional.6
  160.1 1.4 fusion.19
  161.7 1.9 fusion.10
  174.9 66.3 %all-gather.11.cloned.1.call-done = bf16[8192,3,128]{0,2,1:T(8,128)(2,1)} async-done(((bf16[256,3,128]{0,2,1:T(8,128)(2,1)}), bf16[8192,3,128]{0,2,1:T(8,128)(2,1)}) %all-gather.11.cloned.1.call-update) | async-done | bytes 6291472 | tf_op jit(solution)/shard_map/all_gather | solution.py:152
  241.2 8.6 %copy.38 = bf16[8192,3,128]{2,0,1:T(8,128)(2,1)} copy(bf16[8192,3,128]{0,2,1:T(8,128)(2,1)} %all-gather.11.cloned.1.call-done) | data formatting | bytes 12582912
  249.8 61.0 %all-gather.9.cloned.1.call-done = bf16[8192,3,128]{2,0,1:T(8,128)(2,1)} async-done(((bf16[256,3,128]{2,0,1:T(8,128)(2,1)}), bf16[8192,3,128]{2,0,1:T(8,128)(2,1)}) %all-gather.9.cloned.1.call-update) | async-done | bytes 6291472 | tf_op jit(solution)/shard_map/all_gather | solution.py:151
  310.9 89.3 %while.38 = (s32[]{:T(128)}, f32[256,3,128]{0,2,1:T(8,128)S(1)}, f32[256,3,128]{0,2,1:T(8,128)S(1)}, s32[]{:T(128)}, bf16[8192,3,128]{2,0,1:T(8,128)(2,1)}, /*in...) while((s32[]{:T(128)}, f32[256,3,128]{0,2,1:T(8,128)S(1)}, ...), condition=%wide.region_9.10_spmd.clone, body=%wide.region_6.9_spmd.clone.sunk | while | flops 405832448 | bytes 8566113 | solution.py:122
  311.5 4.9 %conditional.7 = ((f32[256,3,128]{0,2,1:T(8,128)S(1)}, f32[256,3,128]{0,2,1:T(8,128)S(1)})) conditional(s32[]{:T(128)} %convert_element_type.71, (f32[256,3,128]{0,2,1:T(8,128)S(1)}, f32[256,3,128]{0,2,1:T(8,128)S(1)}) %tuple.108, (s32[]{:T(128)}, bf16[8192,3,128]{2,0,1:T(8,128)(2,1)}, s32[]{:T(128)}, bf16[256,3,128]{2,0,1:T(8,128)(2,1)S(1)}, ...), branch_computations={%region_7.7_spmd, %region_8.8_spmd} | conditional | flops 405832448 | bytes 8564814 | solution.py:117
  311.8 1.5 subtract_exponential_fusion
  314.7 1.8 fusion.30
  317.1 4.9 %conditional.7 = ((f32[256,3,128]{0,2,1:T(8,128)S(1)}, f32[256,3,128]{0,2,1:T(8,128)S(1)})) conditional(s32[]{:T(128)} %convert_element_type.71, (f32[256,3,128]{0,2,1:T(8,128)S(1)}, f32[256,3,128]{0,2,1:T(8,128)S(1)}) %tuple.108, (s32[]{:T(128)}, bf16[8192,3,128]{2,0,1:T(8,128)(2,1)}, s32[]{:T(128)}, bf16[256,3,128]{2,0,1:T(8,128)(2,1)S(1)}, ...), branch_computations={%region_7.7_spmd, %region_8.8_spmd} | conditional | flops 405832448 | bytes 8564814 | solution.py:117
  317.3 1.5 subtract_exponential_fusion
  320.2 1.8 fusion.30
  322.7 4.9 %conditional.7 = ((f32[256,3,128]{0,2,1:T(8,128)S(1)}, f32[256,3,128]{0,2,1:T(8,128)S(1)})) conditional(s32[]{:T(128)} %convert_element_type.71, (f32[256,3,128]{0,2,1:T(8,128)S(1)}, f32[256,3,128]{0,2,1:T(8,128)S(1)}) %tuple.108, (s32[]{:T(128)}, bf16[8192,3,128]{2,0,1:T(8,128)(2,1)}, s32[]{:T(128)}, bf16[256,3,128]{2,0,1:T(8,128)(2,1)S(1)}, ...), branch_computations={%region_7.7_spmd, %region_8.8_spmd} | conditional | flops 405832448 | bytes 8564814 | solution.py:117
  322.9 1.5 subtract_exponential_fusion
  325.8 1.8 fusion.30
  328.3 4.9 %conditional.7 = ((f32[256,3,128]{0,2,1:T(8,128)S(1)}, f32[256,3,128]{0,2,1:T(8,128)S(1)})) conditional(s32[]{:T(128)} %convert_element_type.71, (f32[256,3,128]{0,2,1:T(8,128)S(1)}, f32[256,3,128]{0,2,1:T(8,128)S(1)}) %tuple.108, (s32[]{:T(128)}, bf16[8192,3,128]{2,0,1:T(8,128)(2,1)}, s32[]{:T(128)}, bf16[256,3,128]{2,0,1:T(8,128)(2,1)S(1)}, ...), branch_computations={%region_7.7_spmd, %region_8.8_spmd} | conditional | flops 405832448 | bytes 8564814 | solution.py:117
  328.5 1.5 subtract_exponential_fusion
  331.4 1.8 fusion.30
  333.9 4.9 %conditional.7 = ((f32[256,3,128]{0,2,1:T(8,128)S(1)}, f32[256,3,128]{0,2,1:T(8,128)S(1)})) conditional(s32[]{:T(128)} %convert_element_type.71, (f32[256,3,128]{0,2,1:T(8,128)S(1)}, f32[256,3,128]{0,2,1:T(8,128)S(1)}) %tuple.108, (s32[]{:T(128)}, bf16[8192,3,128]{2,0,1:T(8,128)(2,1)}, s32[]{:T(128)}, bf16[256,3,128]{2,0,1:T(8,128)(2,1)S(1)}, ...), branch_computations={%region_7.7_spmd, %region_8.8_spmd} | conditional | flops 405832448 | bytes 8564814 | solution.py:117
  334.1 1.5 subtract_exponential_fusion
  335.6 1.4 fusion.27
  337.0 1.8 fusion.30
  339.4 4.9 %conditional.7 = ((f32[256,3,128]{0,2,1:T(8,128)S(1)}, f32[256,3,128]{0,2,1:T(8,128)S(1)})) conditional(s32[]{:T(128)} %convert_element_type.71, (f32[256,3,128]{0,2,1:T(8,128)S(1)}, f32[256,3,128]{0,2,1:T(8,128)S(1)}) %tuple.108, (s32[]{:T(128)}, bf16[8192,3,128]{2,0,1:T(8,128)(2,1)}, s32[]{:T(128)}, bf16[256,3,128]{2,0,1:T(8,128)(2,1)S(1)}, ...), branch_computations={%region_7.7_spmd, %region_8.8_spmd} | conditional | flops 405832448 | bytes 8564814 | solution.py:117
  339.7 1.5 subtract_exponential_fusion
  341.2 1.4 fusion.27
  342.6 1.8 fusion.30
  345.0 4.9 %conditional.7 = ((f32[256,3,128]{0,2,1:T(8,128)S(1)}, f32[256,3,128]{0,2,1:T(8,128)S(1)})) conditional(s32[]{:T(128)} %convert_element_type.71, (f32[256,3,128]{0,2,1:T(8,128)S(1)}, f32[256,3,128]{0,2,1:T(8,128)S(1)}) %tuple.108, (s32[]{:T(128)}, bf16[8192,3,128]{2,0,1:T(8,128)(2,1)}, s32[]{:T(128)}, bf16[256,3,128]{2,0,1:T(8,128)(2,1)S(1)}, ...), branch_computations={%region_7.7_spmd, %region_8.8_spmd} | conditional | flops 405832448 | bytes 8564814 | solution.py:117
  345.2 1.5 subtract_exponential_fusion
  348.1 1.8 fusion.30
  350.6 4.9 %conditional.7 = ((f32[256,3,128]{0,2,1:T(8,128)S(1)}, f32[256,3,128]{0,2,1:T(8,128)S(1)})) conditional(s32[]{:T(128)} %convert_element_type.71, (f32[256,3,128]{0,2,1:T(8,128)S(1)}, f32[256,3,128]{0,2,1:T(8,128)S(1)}) %tuple.108, (s32[]{:T(128)}, bf16[8192,3,128]{2,0,1:T(8,128)(2,1)}, s32[]{:T(128)}, bf16[256,3,128]{2,0,1:T(8,128)(2,1)S(1)}, ...), branch_computations={%region_7.7_spmd, %region_8.8_spmd} | conditional | flops 405832448 | bytes 8564814 | solution.py:117
  350.8 1.5 subtract_exponential_fusion
  353.7 1.8 fusion.30
  356.2 4.9 %conditional.7 = ((f32[256,3,128]{0,2,1:T(8,128)S(1)}, f32[256,3,128]{0,2,1:T(8,128)S(1)})) conditional(s32[]{:T(128)} %convert_element_type.71, (f32[256,3,128]{0,2,1:T(8,128)S(1)}, f32[256,3,128]{0,2,1:T(8,128)S(1)}) %tuple.108, (s32[]{:T(128)}, bf16[8192,3,128]{2,0,1:T(8,128)(2,1)}, s32[]{:T(128)}, bf16[256,3,128]{2,0,1:T(8,128)(2,1)S(1)}, ...), branch_computations={%region_7.7_spmd, %region_8.8_spmd} | conditional | flops 405832448 | bytes 8564814 | solution.py:117
  356.4 1.5 subtract_exponential_fusion
  359.3 1.8 fusion.30
  361.8 4.9 %conditional.7 = ((f32[256,3,128]{0,2,1:T(8,128)S(1)}, f32[256,3,128]{0,2,1:T(8,128)S(1)})) conditional(s32[]{:T(128)} %convert_element_type.71, (f32[256,3,128]{0,2,1:T(8,128)S(1)}, f32[256,3,128]{0,2,1:T(8,128)S(1)}) %tuple.108, (s32[]{:T(128)}, bf16[8192,3,128]{2,0,1:T(8,128)(2,1)}, s32[]{:T(128)}, bf16[256,3,128]{2,0,1:T(8,128)(2,1)S(1)}, ...), branch_computations={%region_7.7_spmd, %region_8.8_spmd} | conditional | flops 405832448 | bytes 8564814 | solution.py:117
  362.0 1.5 subtract_exponential_fusion
  364.9 1.8 fusion.30
  367.4 4.9 %conditional.7 = ((f32[256,3,128]{0,2,1:T(8,128)S(1)}, f32[256,3,128]{0,2,1:T(8,128)S(1)})) conditional(s32[]{:T(128)} %convert_element_type.71, (f32[256,3,128]{0,2,1:T(8,128)S(1)}, f32[256,3,128]{0,2,1:T(8,128)S(1)}) %tuple.108, (s32[]{:T(128)}, bf16[8192,3,128]{2,0,1:T(8,128)(2,1)}, s32[]{:T(128)}, bf16[256,3,128]{2,0,1:T(8,128)(2,1)S(1)}, ...), branch_computations={%region_7.7_spmd, %region_8.8_spmd} | conditional | flops 405832448 | bytes 8564814 | solution.py:117
  367.6 1.5 subtract_exponential_fusion
  370.5 1.8 fusion.30
  372.9 4.9 %conditional.7 = ((f32[256,3,128]{0,2,1:T(8,128)S(1)}, f32[256,3,128]{0,2,1:T(8,128)S(1)})) conditional(s32[]{:T(128)} %convert_element_type.71, (f32[256,3,128]{0,2,1:T(8,128)S(1)}, f32[256,3,128]{0,2,1:T(8,128)S(1)}) %tuple.108, (s32[]{:T(128)}, bf16[8192,3,128]{2,0,1:T(8,128)(2,1)}, s32[]{:T(128)}, bf16[256,3,128]{2,0,1:T(8,128)(2,1)S(1)}, ...), branch_computations={%region_7.7_spmd, %region_8.8_spmd} | conditional | flops 405832448 | bytes 8564814 | solution.py:117
  373.2 1.5 subtract_exponential_fusion
  376.1 1.8 fusion.30
  378.5 4.9 %conditional.7 = ((f32[256,3,128]{0,2,1:T(8,128)S(1)}, f32[256,3,128]{0,2,1:T(8,128)S(1)})) conditional(s32[]{:T(128)} %convert_element_type.71, (f32[256,3,128]{0,2,1:T(8,128)S(1)}, f32[256,3,128]{0,2,1:T(8,128)S(1)}) %tuple.108, (s32[]{:T(128)}, bf16[8192,3,128]{2,0,1:T(8,128)(2,1)}, s32[]{:T(128)}, bf16[256,3,128]{2,0,1:T(8,128)(2,1)S(1)}, ...), branch_computations={%region_7.7_spmd, %region_8.8_spmd} | conditional | flops 405832448 | bytes 8564814 | solution.py:117
  378.7 1.5 subtract_exponential_fusion
  381.6 1.8 fusion.30
  384.1 4.9 %conditional.7 = ((f32[256,3,128]{0,2,1:T(8,128)S(1)}, f32[256,3,128]{0,2,1:T(8,128)S(1)})) conditional(s32[]{:T(128)} %convert_element_type.71, (f32[256,3,128]{0,2,1:T(8,128)S(1)}, f32[256,3,128]{0,2,1:T(8,128)S(1)}) %tuple.108, (s32[]{:T(128)}, bf16[8192,3,128]{2,0,1:T(8,128)(2,1)}, s32[]{:T(128)}, bf16[256,3,128]{2,0,1:T(8,128)(2,1)S(1)}, ...), branch_computations={%region_7.7_spmd, %region_8.8_spmd} | conditional | flops 405832448 | bytes 8564814 | solution.py:117
  384.3 1.5 subtract_exponential_fusion
  385.9 1.4 fusion.27
  387.2 1.8 fusion.30
  389.7 4.9 %conditional.7 = ((f32[256,3,128]{0,2,1:T(8,128)S(1)}, f32[256,3,128]{0,2,1:T(8,128)S(1)})) conditional(s32[]{:T(128)} %convert_element_type.71, (f32[256,3,128]{0,2,1:T(8,128)S(1)}, f32[256,3,128]{0,2,1:T(8,128)S(1)}) %tuple.108, (s32[]{:T(128)}, bf16[8192,3,128]{2,0,1:T(8,128)(2,1)}, s32[]{:T(128)}, bf16[256,3,128]{2,0,1:T(8,128)(2,1)S(1)}, ...), branch_computations={%region_7.7_spmd, %region_8.8_spmd} | conditional | flops 405832448 | bytes 8564814 | solution.py:117
  389.9 1.5 subtract_exponential_fusion
  392.8 1.8 fusion.30
  395.3 4.9 %conditional.7 = ((f32[256,3,128]{0,2,1:T(8,128)S(1)}, f32[256,3,128]{0,2,1:T(8,128)S(1)})) conditional(s32[]{:T(128)} %convert_element_type.71, (f32[256,3,128]{0,2,1:T(8,128)S(1)}, f32[256,3,128]{0,2,1:T(8,128)S(1)}) %tuple.108, (s32[]{:T(128)}, bf16[8192,3,128]{2,0,1:T(8,128)(2,1)}, s32[]{:T(128)}, bf16[256,3,128]{2,0,1:T(8,128)(2,1)S(1)}, ...), branch_computations={%region_7.7_spmd, %region_8.8_spmd} | conditional | flops 405832448 | bytes 8564814 | solution.py:117
  395.5 1.5 subtract_exponential_fusion
  398.4 1.8 fusion.30
  (162 shorter events, 31.0 us)
Async XLA Ops:
  7.2 143.8 %all-gather.5.cloned.1.call-start = ((), (), s32[]{:S(2)}) async-start(), calls=%async_computation.1 | async-start | bytes 6488064 | tf_op jit(solution)/shard_map/all_gather | solution.py:143
  7.9 151.5 %all-gather.7.cloned.1.call-start = ((), (), s32[]{:S(2)}) async-start(), calls=%async_computation.2 | async-start | bytes 6488064 | tf_op jit(solution)/shard_map/all_gather | solution.py:144
  8.6 232.6 %all-gather.11.cloned.1.call-start = ((), (), s32[]{:S(2)}) async-start(), calls=%async_computation.4 | async-start | bytes 6488064 | tf_op jit(solution)/shard_map/all_gather | solution.py:152
  10.0 58.8 %copy-start.5 = (bf16[384,5120]{1,0:T(8,128)(2,1)S(1)}, bf16[384,5120]{1,0:T(8,128)(2,1)}, u32[]{:S(2)}) copy-start(bf16[384,5120]{1,0:T(8,128)(2,1)} %param.20) | copy-start | bytes 11796484
  68.9 4.3 %copy-start.4 = (f32[256,3]{0,1:T(4,128)S(1)}, f32[256,3]{0,1:T(4,128)}, u32[]{:S(2)}) copy-start(f32[256,3]{0,1:T(4,128)} %param.21) | copy-start | bytes 9220
  70.4 49.0 %copy-start.3 = (bf16[256,3,128]{2,0,1:T(8,128)(2,1)S(1)}, bf16[256,3,128]{2,0,1:T(8,128)(2,1)}, u32[]{:S(2)}) copy-start(bf16[256,3,128]{2,0,1:T(8,128)(2,1)} %param.18) | copy-start | bytes 589828
  70.5 89.0 %copy-start = (bf16[256,3,128]{2,0,1:T(8,128)(2,1)S(1)}, bf16[256,3,128]{2,0,1:T(8,128)(2,1)}, u32[]{:S(2)}) copy-start(bf16[256,3,128]{2,0,1:T(8,128)(2,1)} %param.15) | copy-start | bytes 589828
  71.3 239.5 %all-gather.9.cloned.1.call-start = ((), (), s32[]{:S(2)}) async-start(), calls=%async_computation.3 | async-start | bytes 6488064 | tf_op jit(solution)/shard_map/all_gather | solution.py:151
  174.9 136.0 %copy-start.1 = (bf16[256,3,128]{2,0,1:T(8,128)(2,1)S(1)}, bf16[256,3,128]{2,0,1:T(8,128)(2,1)}, u32[]{:S(2)}) copy-start(bf16[256,3,128]{2,0,1:T(8,128)(2,1)} %param.17) | copy-start | bytes 589828
  174.9 136.0 %copy-start.2 = (bf16[256,3,128]{2,0,1:T(8,128)(2,1)S(1)}, bf16[256,3,128]{2,0,1:T(8,128)(2,1)}, u32[]{:S(2)}) copy-start(bf16[256,3,128]{2,0,1:T(8,128)(2,1)} %param.16) | copy-start | bytes 589828
Sparse Core Ops, SparseCore 0:
  9.8 77.3 all-gather.4
  89.1 70.2 all-gather.6
  161.7 79.4 all-gather.10
  242.9 67.8 all-gather.8
